TPU v7x, 32 devices: a whole 2x2x4 slice. The times are simulated.
32 devices in a mesh: parts: 2 (over x), seq: 16 (over z, y, core).
Axes of the slice: x: 2, y: 2, z: 4, core: 2. Of those that a mesh axis runs over, the one named last changes fastest.
Arguments:
- conv_input: bfloat16 [32768, 2816], P(('parts', 'seq')), parts along dimension 0, may hold values from -6 to 6
- step_raw: bfloat16 [32768, 40], P(('parts', 'seq')), parts along dimension 0, may hold values from -4 to 4
- conv_weight: float32 [4, 2816], replicated, may hold values from -3 to 3
- conv_bias: float32 [2816], replicated, may hold values from -3 to 3
- step_bias: float32 [40], replicated, may hold values from -1 to 1
- decay_rate: float32 [40], replicated, may hold values from 1.8310547e-07 to 0.05, as said below
- norm_gain: float32 [2560], replicated, may hold values from 0.1 to 1.9
Outputs:
- layer_out: bfloat16 [32768, 2560], P(('parts', 'seq')), parts along dimension 0
There are 2 independent parts, one for each index of `parts`. A program takes and returns all parts, laid end to end along the dimension named above; an argument that names none is the same for every part. Nothing has to cross between parts.
Inputs may be any that keep to these rules, and one draw needn't show every extreme that they name: `decay_rate`: positive decay rates, one per head.
All inputs are finite; a program needn't handle non-finite values.
Results may differ from a plain program's by a relative error of at most 0.0034.
Values may be sent and summed in bfloat16 or wider, within the bound.
A program may use at most 384 MiB of HBM per device.

v0:
```python
import jax
import jax.numpy as jnp
from jax import lax
from jax.sharding import PartitionSpec as P

GROUP = 256


def entering(array, axis, combine, identity):
    devices, place = (lax.axis_size(axis), lax.axis_index(axis))
    everything = jax.tree.map(lambda part: lax.all_gather(part, axis), array)
    start = jax.tree.map(
        lambda part, zero: jnp.broadcast_to(jnp.asarray(zero, part.dtype), part.shape),
        array,
        identity,
    )

    def lap(k, before):
        reached = k < place
        new = combine(before, jax.tree.map(lambda part: part[k], everything))
        return jax.tree.map(lambda a, b: jnp.where(reached, a, b), new, before)

    return lax.fori_loop(0, devices, lap, start)


def from_behind(value, axis, steps):
    count = lax.axis_size(axis)
    initial, last = (max(0, -steps), min(count, count - steps))
    return lax.ppermute(value, axis, [(source, source + steps) for source in range(initial, last)])


def conv_mix(padded, conv_weight, conv_bias, row_count):
    total = jnp.zeros((row_count, padded.shape[1]), jnp.float32) + conv_bias
    for offset in range(conv_weight.shape[0]):
        total = (
            total + padded[offset : offset + row_count].astype(jnp.float32) * conv_weight[offset]
        )
    return jax.nn.silu(total).astype(jnp.bfloat16)


def block_parts(values, inputs_b, inputs_c, step_sizes, log_decay):
    cumulative = jnp.cumsum(log_decay, axis=0)
    scores = jnp.dot(inputs_c, inputs_b.T, preferred_element_type=jnp.float32)
    span_rows = log_decay.shape[0]
    causal = jnp.tril(jnp.ones((span_rows, span_rows), dtype=bool))
    gap_table = cumulative.T[:, :, None] - cumulative.T[:, None, :]
    decay = jnp.where(causal[None], jnp.exp(jnp.where(causal[None], gap_table, 0.0)), 0.0)
    mixing = (scores[None] * decay * step_sizes.T[:, None, :]).astype(jnp.bfloat16)
    within = jnp.einsum("hts,shp->thp", mixing, values, preferred_element_type=jnp.float32)
    weights = jnp.exp(cumulative[-1][None, :] - cumulative) * step_sizes
    scaled = (weights[:, :, None] * values.astype(jnp.float32)).astype(jnp.bfloat16)
    update = jnp.einsum("shp,sn->hpn", scaled, inputs_b, preferred_element_type=jnp.float32)
    return (cumulative, within, update)


def chain_states(start_state, block_ends, updates):

    def advance(carried, pieces):
        factor, update = pieces
        return (factor[:, None, None] * carried + update, carried)

    return lax.scan(advance, start_state, (block_ends, updates))


def read_states(previous, inputs_c, cumulative):
    across = jnp.einsum(
        "khpn,kqn->kqhp", previous, inputs_c.astype(jnp.float32), precision=lax.Precision.HIGHEST
    )
    return across * jnp.exp(cumulative)[..., None]


def combine_states(earlier, later):
    return (earlier[0] * later[0], earlier[1] * later[0][:, None, None] + later[1])


def hand_off(device_decay, local_final):
    identity = (jnp.ones_like(device_decay), jnp.zeros_like(local_final))
    prefix = entering((device_decay, local_final), "seq", combine_states, identity)
    return prefix[1]


def finish(result, norm_gain):
    flat = result.reshape(-1, norm_gain.shape[0])
    scale = lax.rsqrt(jnp.mean(flat * flat, axis=-1, keepdims=True) + 1e-05)
    return (flat * scale * norm_gain).astype(jnp.bfloat16)


def per_device(conv_input, step_raw, conv_weight, conv_bias, step_bias, decay_rate, norm_gain):
    token_rows, conv_dim = conv_input.shape
    head_count = decay_rate.shape[0]
    inner = norm_gain.shape[0]
    state_dim = (conv_dim - inner) // 2
    head_size = inner // head_count
    margin = conv_weight.shape[0] - 1
    upper_rows = from_behind(conv_input[token_rows - margin :], "seq", 1)
    mixed = conv_mix(
        jnp.concatenate([upper_rows, conv_input], axis=0), conv_weight, conv_bias, token_rows
    )
    step_sizes = jax.nn.softplus(step_raw.astype(jnp.float32) + step_bias)
    log_decay = -decay_rate * step_sizes
    blocks = token_rows // GROUP
    values = mixed[:, :inner].reshape(blocks, GROUP, head_count, head_size)
    inputs_b = mixed[:, inner : inner + state_dim].reshape(blocks, GROUP, state_dim)
    inputs_c = mixed[:, inner + state_dim :].reshape(blocks, GROUP, state_dim)
    block_steps = step_sizes.reshape(blocks, GROUP, head_count)
    block_logs = log_decay.reshape(blocks, GROUP, head_count)
    cumulative, within, updates = lax.map(
        lambda pieces: block_parts(*pieces), (values, inputs_b, inputs_c, block_steps, block_logs)
    )
    block_ends = jnp.exp(cumulative[:, -1])
    zero_state = jnp.zeros((head_count, head_size, state_dim), jnp.float32)
    local_final, local_previous = chain_states(zero_state, block_ends, updates)
    device_decay = jnp.prod(block_ends, axis=0)
    incoming = hand_off(device_decay, local_final)
    unused_final, previous = chain_states(incoming, block_ends, updates)
    across = read_states(previous, inputs_c, cumulative)
    return finish(within + across, norm_gain)


def solution(mesh):
    placed = (P(("parts", "seq"), None), P(("parts", "seq"), None), P(), P(), P(), P(), P())
    return jax.shard_map(
        per_device, mesh=mesh, in_specs=placed, out_specs=P(("parts", "seq"), None), check_vma=False
    )
```

profile of v0, /device:TPU:0, one launch (start us, length us, event | category | flops | bytes accessed | tf_op | source)
XLA Modules:
  0.0 314.3 jit_solution(15832321208408284778)
XLA Ops:
  12.8 13.5 %multiply_convert_fusion.5 = bf16[1024,2816]{1,0:T(8,128)(2,1)S(1)} fusion(bf16[1024,2816]{1,0:T(8,128)(2,1)} %param.15, bf16[3,2816]{1,0:T(4,128)(2,1)S(1)} %collective-permute-done, f32[2816]{0:T(1024)S(1)} %get-tuple-element.265, f32[2816]{0:T(1024)S(1)} %get-tuple-element.266, f32[2816]{0:T(1024)S(1)} %get-tuple-element.264, ...), kind=kLoop, calls=%fused_computation.51 | loop fusion | flops 74973184 | bytes 11607552 | tf_op jit(solution)/shard_map/convert_element_type | solution.py:38
  29.0 13.7 %reshape.103 = bf16[4,256,40,64]{3,2,1,0:T(8,128)(2,1)} reshape(bf16[1024,2560]{1,0:T(8,128)(2,1)} %slice.63) | data formatting | bytes 10485760 | tf_op jit(solution)/shard_map/reshape | solution.py:102
  42.7 11.1 %copy.36 = bf16[4,256,40,64]{1,3,2,0:T(8,128)(2,1)} copy(bf16[4,256,40,64]{3,2,1,0:T(8,128)(2,1)} %reshape.103) | data formatting | bytes 10485760 | tf_op jit(solution)/shard_map/while | solution.py:107
  53.8 3.0 broadcast.39.clone
  56.8 40.3 %while.51 = (s32[]{:T(128)}, f32[4,256,40]{1,2,0:T(8,128)S(1)}, f32[4,256,40,64]{1,3,2,0:T(8,128)}, f32[4,40,64,128]{3,2,1,0:T(8,128)}, f32[4,256,40]{1,0,2:T(4,...) while((s32[]{:T(128)}, f32[4,256,40]{1,2,0:T(8,128)S(1)}, ...), condition=%wide.region_3.4_spmd, body=%wide.region_0.3_spmd.sunk | while | flops 539205760 | bytes 8314621 | solution.py:107
  58.1 5.6 %bitcast_dynamic-update-slice_fusion.7 = f32[4,256,40,64]{1,3,2,0:T(8,128)} fusion(f32[4,256,40,64]{1,3,2,0:T(8,128)} %get-tuple-element.488, s32[]{:T(128)} %get-tuple-element.486, f32[40,256]{1,0:T(8,128)S(1)} %bitcast.156, f32[40,256]{1,0:T(8,128)S(1)} %get-tuple-element.459, f32[256,256]{1,0:T(8,128)S(1)} %fusion.51, ...), kind=kOutput, calls=%fused_computation.18.clone.1 | convolution fusion | flops 351272960 | bytes 4383744 | tf_op jit(solution)/shard_map/while/body/eval_jaxpr/hts,shp->thp/dot_general | solution.py:49
  64.0 2.9 fusion.52
  68.2 5.6 %bitcast_dynamic-update-slice_fusion.7 = f32[4,256,40,64]{1,3,2,0:T(8,128)} fusion(f32[4,256,40,64]{1,3,2,0:T(8,128)} %get-tuple-element.488, s32[]{:T(128)} %get-tuple-element.486, f32[40,256]{1,0:T(8,128)S(1)} %bitcast.156, f32[40,256]{1,0:T(8,128)S(1)} %get-tuple-element.459, f32[256,256]{1,0:T(8,128)S(1)} %fusion.51, ...), kind=kOutput, calls=%fused_computation.18.clone.1 | convolution fusion | flops 351272960 | bytes 4383744 | tf_op jit(solution)/shard_map/while/body/eval_jaxpr/hts,shp->thp/dot_general | solution.py:49
  74.1 2.9 fusion.52
  78.3 5.5 %bitcast_dynamic-update-slice_fusion.7 = f32[4,256,40,64]{1,3,2,0:T(8,128)} fusion(f32[4,256,40,64]{1,3,2,0:T(8,128)} %get-tuple-element.488, s32[]{:T(128)} %get-tuple-element.486, f32[40,256]{1,0:T(8,128)S(1)} %bitcast.156, f32[40,256]{1,0:T(8,128)S(1)} %get-tuple-element.459, f32[256,256]{1,0:T(8,128)S(1)} %fusion.51, ...), kind=kOutput, calls=%fused_computation.18.clone.1 | convolution fusion | flops 351272960 | bytes 4383744 | tf_op jit(solution)/shard_map/while/body/eval_jaxpr/hts,shp->thp/dot_general | solution.py:49
  84.1 2.9 fusion.52
  88.3 5.5 %bitcast_dynamic-update-slice_fusion.7 = f32[4,256,40,64]{1,3,2,0:T(8,128)} fusion(f32[4,256,40,64]{1,3,2,0:T(8,128)} %get-tuple-element.488, s32[]{:T(128)} %get-tuple-element.486, f32[40,256]{1,0:T(8,128)S(1)} %bitcast.156, f32[40,256]{1,0:T(8,128)S(1)} %get-tuple-element.459, f32[256,256]{1,0:T(8,128)S(1)} %fusion.51, ...), kind=kOutput, calls=%fused_computation.18.clone.1 | convolution fusion | flops 351272960 | bytes 4383744 | tf_op jit(solution)/shard_map/while/body/eval_jaxpr/hts,shp->thp/dot_general | solution.py:49
  94.2 2.9 fusion.52
  97.4 6.3 %while.53 = (s32[]{:T(128)}, f32[40,64,128]{2,1,0:T(8,128)S(1)}, f32[4,40]{1,0:T(4,128)S(1)}, f32[4,40,64,128]{3,2,1,0:T(8,128)}, s32[]{:T(128)}, /*index=5*/s32[]{:T(128)}) while((s32[]{:T(128)}, f32[40,64,128]{2,1,0:T(8,128)S(1)}, f32[4,40]{1,0:T(4,128)S(1)}, f32[4,40,64,128]{3,2,1,0:T(8,128)}, s32[]{:T(128)}, ...), condition=%wide.region_6.7_spmd.clone, body=%wide.region_5.6_spmd.clone.sunk | while | flops 983043 | bytes 3932727 | solution.py:62
  106.5 35.2 %all-reduce = f32[640]{0:T(1024)S(1)} all-reduce(f32[640]{0:T(1024)S(1)} %dynamic-update-slice), channel_id=2, replica_groups=mesh['parts'=2,'seq'=16] {'seq'}, use_global_device_ids=true, to_apply=%add | all-reduce | flops 640 | bytes 5120
  141.8 74.8 %all-gather.4.cloned.1.call-done = f32[640,64,128]{2,1,0:T(8,128)} async-done(((f32[40,64,128]{2,1,0:T(8,128)}), f32[640,64,128]{2,1,0:T(8,128)}) %all-gather.4.cloned.1.call-update) | async-done | bytes 20971536 | tf_op jit(solution)/shard_map/all_gather | solution.py:11
  216.6 26.5 %while.54 = (s32[]{:T(128)}, f32[40,64,128]{2,1,0:T(8,128)S(1)}, s32[]{:T(128)}, f32[16,40]{1,0:T(8,128)S(1)}, f32[16,40,64,128]{3,2,1,0:T(8,128)}, /*index=5*/s32[]{:T(128)}, s32[]{:T(128)}) while((s32[]{:T(128)}, f32[40,64,128]{2,1,0:T(8,128)S(1)}, s32[]{:T(128)}, f32[16,40]{1,0:T(8,128)S(1)}, f32[16,40,64,128]{3,2,1,0:T(8,128)}, ...), condition=%wide.region_8.9_spmd.clone, body=%wide.region_7.8_spmd.clone.sunk | while | flops 1310724 | bytes 3932745 | solution.py:23
  243.1 3.0 broadcast.39
  246.2 11.2 %while.52 = (s32[]{:T(128)}, f32[40,64,128]{2,1,0:T(8,128)S(1)}, f32[4,40,64,128]{3,2,1,0:T(8,128)}, f32[4,40]{1,0:T(4,128)S(1)}, f32[4,40,64,128]{3,2,1,0:T(8,128)}, /*index=5*/s32[]{:T(128)}) while((s32[]{:T(128)}, f32[40,64,128]{2,1,0:T(8,128)S(1)}, f32[4,40,64,128]{3,2,1,0:T(8,128)}, f32[4,40]{1,0:T(4,128)S(1)}, ...), condition=%wide.region_10.11_spmd, body=%wide.region_9.10_spmd.sunk | while | flops 655362 | bytes 6554669 | solution.py:62
  257.4 14.8 %multiply_reduce_fusion = (f32[4,256]{1,0:T(4,128)S(1)}, f32[4,256,40,64]{1,3,2,0:T(8,128)}) fusion(f32[4,256,40,64]{1,3,2,0:T(8,128)} %get-tuple-element.197, f32[4,256,40]{1,2,0:T(8,128)S(1)} %exp.27, bf16[4,256,128,1]{2,1,3,0:T(8,128)(2,1)S(1)} %bitcast.154, f32[4,40,64,128]{3,2,1,0:T(8,128)} %get-tuple-element.202), kind=kOutput, calls=%fused_computation.53 | convolution fusion | flops 4037016576 | bytes 26644480 | tf_op jit(solution)/shard_map/khpn,kqn->kqhp/dot_general | solution.py:66
  272.2 17.4 %copy.39 = f32[4,256,40,64]{1,0,3,2:T(4,128)} copy(f32[4,256,40,64]{1,3,2,0:T(8,128)} %get-tuple-element.324) | data formatting | bytes 20971520 | tf_op jit(solution)/shard_map/add | solution.py:117
  289.6 6.6 %copy.48 = f32[320,8,4,256]{3,1,2,0:T(8,128)S(1)} copy(f32[320,8,4,256]{3,2,1,0:T(4,128)} %bitcast.151) | data formatting | bytes 20971520
  296.2 3.3 %multiply_convert_fusion.6 = bf16[1024,2560]{0,1:T(8,128)(2,1)} fusion(f32[1024,2560]{0,1:T(8,128)S(1)} %bitcast.150, f32[2560]{0:T(1024)S(1)} %copy-done.1, f32[1024]{0:T(1024)S(1)} %bitcast.157), kind=kLoop, calls=%fused_computation.52 | loop fusion | flops 7864320 | bytes 15742976 | tf_op jit(solution)/shard_map/convert_element_type | solution.py:85
  299.5 7.9 %copy.40 = bf16[1024,2560]{1,0:T(8,128)(2,1)} copy(bf16[1024,2560]{0,1:T(8,128)(2,1)} %multiply_convert_fusion.6) | data formatting | bytes 10485760 | tf_op jit(solution)/shard_map/convert_element_type | solution.py:85
  (135 shorter events, 60.7 us)
Async XLA Ops:
  6.5 210.1 %all-gather.4.cloned.1.call-start = ((), (), s32[]{:S(2)}) async-start(), calls=%async_computation | async-start | bytes 22282240 | tf_op jit(solution)/shard_map/all_gather | solution.py:11
  7.3 5.4 %collective-permute-start = (bf16[3,2816]{1,0:T(4,128)(2,1)S(1)}, bf16[3,2816]{1,0:T(4,128)(2,1)S(1)}, u32[]{:S(2)}, u32[]{:S(2)}) collective-permute-start(bf16[3,2816]{1,0:T(4,128)(2,1)S(1)} %slice.45), channel_id=1, source_target_pairs={{0,1},{1,2},{2,3},{3,4},{4,5},{5,6},{6,7},{7,8},{8,9},{9,10},{10,1... | collective-permute-start | bytes 50696 | tf_op jit(solution)/shard_map/ppermute | solution.py:29
  97.4 7.4 %copy-start.2 = (u32[32]{0:T(128)S(1)}, u32[32]{0:T(128)}, u32[]{:S(2)}) copy-start(u32[32]{0:T(128)} %constant.91) | copy-start | bytes 388
  103.7 1.1 copy-start
  289.6 6.6 %copy-start.1 = (f32[2560]{0:T(1024)S(1)}, f32[2560]{0:T(1024)}, u32[]{:S(2)}) copy-start(f32[2560]{0:T(1024)} %param.21) | copy-start | bytes 30724
Sparse Core Ops, SparseCore 0:
  104.9 111.6 all-gather.3
where the time goes:
time: 316 us; the launch traced here: 314 us
  local copies, waits for them, and re-layouts  76.6 us (24%)
  waiting for transfers between devices  74.8 us (24%)
  other arithmetic  60.4 us (19%)
  matrix products  49.5 us (16%)
  blocking collectives  35.2 us (11%)
  between operations  14.3 us (5%)
    all_gather x1, waiting for transfers between devices, entering(): everything = jax.tree.map(lambda part: lax.all_gather(part, axis), array)  74.8 us
    unnamed x1, blocking collectives  35.2 us
    select_n x16, other arithmetic, lap(): return jax.tree.map(lambda a, b: jnp.where(reached, a, b), new, before)  25.9 us
    dot_general x4, matrix products, block_parts(): jnp.einsum('hts,shp->thp', mixing, values, preferred_element_type=jnp.flo...  22.3 us
    add x1, local copies, waits for them, and re-layouts, per_device(): return finish(within + across, norm_gain)  17.4 us
    dot_general x1, matrix products, read_states(): jnp.einsum('khpn,kqn->kqhp', previous, inputs_c.astype(jnp.float32), prec...  14.8 us
    reshape x1, local copies, waits for them, and re-layouts, per_device(): values = mixed[:, :inner].reshape(blocks, GROUP, head_count, head_size)  13.7 us
    convert_element_type x1, other arithmetic, conv_mix(): return jax.nn.silu(total).astype(jnp.bfloat16)  13.5 us
  transfers between devices with their start and end apart: 2, of which 1 were waited for; matrix products, arithmetic and copies ran while one was open for 1% of the time, Pallas kernels for 0%

commit v1 on v0

v1 whole, which is shorter than its diff:
```python
import functools

import jax
import jax.numpy as jnp
from jax import lax
from jax.experimental import pallas as pl
from jax.experimental.pallas import tpu as pltpu
from jax.sharding import PartitionSpec as P

GROUP = 256
WIDE = 256
HALO = 8
F32, BF16 = jnp.float32, jnp.bfloat16


def dot(left, right):
    return jnp.dot(left, right, preferred_element_type=F32)


def split(value):
    high = value.astype(BF16).astype(F32)
    return high, value - high


def lower_triangle():
    rows = lax.broadcasted_iota(jnp.int32, (GROUP, GROUP), 0)
    columns = lax.broadcasted_iota(jnp.int32, (GROUP, GROUP), 1)
    return rows >= columns


def front_kernel(
    inner, heads,
    before_ref, input_ref, raw_ref, weight_ref, bias_ref, step_bias_ref, rate_ref, spread_ref,
    xb_ref, bc_ref, a_ref, g_ref, state_ref, decay_ref,
    buf, pack,
):
    block = pl.program_id(0)

    @pl.when(block == 0)
    def _():
        buf[0:HALO] = before_ref[...].astype(F32)
        pack[...] = jnp.zeros_like(pack)
        state_ref[...] = jnp.zeros_like(state_ref)
        decay_ref[...] = jnp.ones_like(decay_ref)

    @pl.when(block > 0)
    def _():
        buf[0:HALO] = buf[GROUP : GROUP + HALO]

    half = pack.shape[1] // 2

    def packed(value):
        high, low = split(value)
        rows = value.shape[0]
        pack[0:rows, 0:heads] = high
        pack[0:rows, half : half + heads] = low
        return pack[0:rows, :].astype(BF16)

    shifted = raw_ref[...].astype(F32) + step_bias_ref[...]
    step = jnp.maximum(shifted, 0.0) + jnp.log(1.0 + jnp.exp(-jnp.abs(shifted)))
    logs = -rate_ref[...] * step
    ones = lower_triangle().astype(BF16)
    high, rest = split(logs)
    middle, low = split(rest)
    cum = dot(ones, high.astype(BF16)) + (
        dot(ones, middle.astype(BF16)) + dot(ones, low.astype(BF16))
    )
    mid = 0.5 * cum[GROUP - 1 : GROUP]
    a_ref[...] = packed(jnp.exp(cum - mid))
    g_pack = packed(jnp.exp(jnp.broadcast_to(mid, (8, heads))))
    b_pack = packed(jnp.exp(mid - cum) * step)

    def mix(columns):
        buf[HALO : HALO + GROUP, columns] = input_ref[:, columns].astype(F32)
        total = bias_ref[:, columns] + buf[HALO - 3 : HALO - 3 + GROUP, columns] * weight_ref[0:1, columns]
        for k in range(1, 4):
            total = total + buf[HALO - 3 + k : HALO - 3 + k + GROUP, columns] * weight_ref[k : k + 1, columns]
        part = 0.5 * total
        return (part + part * jnp.tanh(part)).astype(BF16)

    bc = mix(slice(inner, inner + WIDE))
    bc_ref[...] = bc
    b_turned = bc[:, : WIDE // 2].astype(F32).T.astype(BF16)

    for j in range(inner // WIDE):
        columns = slice(j * WIDE, (j + 1) * WIDE)
        spread = spread_ref[:, columns]
        xb = (mix(columns).astype(F32) * dot(b_pack, spread)).astype(BF16)
        xb_ref[:, columns] = xb
        g8 = dot(g_pack, spread)
        g_ref[:, columns] = g8
        g = g8[0:1]
        state_ref[:, columns] = g * (g * state_ref[:, columns] + dot(b_turned, xb))
        decay_ref[:, columns] = decay_ref[:, columns] * (g8 * g8)


def back_kernel(
    inner,
    xb_ref, bc_ref, a_ref, g_ref, spread_ref, incoming_ref, gain_ref,
    out_ref,
    state, rows,
):
    @pl.when(pl.program_id(0) == 0)
    def _():
        state[...] = incoming_ref[...].astype(F32)

    bc = bc_ref[...]
    width = WIDE // 2
    b, c = bc[:, :width], bc[:, width:]
    b_turned = b.astype(F32).T.astype(BF16)
    scores = dot(c, b_turned)
    scores = jnp.where(lower_triangle(), scores, 0.0).astype(BF16)
    c_twice = jnp.concatenate([c, c], axis=1)
    a_pack = a_ref[...]
    squares = jnp.zeros((GROUP, WIDE), F32)
    for j in range(inner // WIDE):
        columns = slice(j * WIDE, (j + 1) * WIDE)
        xb = xb_ref[:, columns]
        g = g_ref[0:1, columns]
        held = g * state[:, columns]
        high = held.astype(BF16)
        low = (held - high.astype(F32)).astype(BF16)
        total = dot(scores, xb) + dot(c_twice, jnp.concatenate([high, low], axis=0))
        y = total * dot(a_pack, spread_ref[:, columns])
        rows[:, columns] = y
        squares = squares + y * y
        state[:, columns] = g * (held + dot(b_turned, xb))
    mean = jnp.sum(squares, axis=1, keepdims=True) * (1.0 / inner)
    scale = lax.rsqrt(mean + 1e-05)
    for j in range(inner // WIDE):
        columns = slice(j * WIDE, (j + 1) * WIDE)
        out_ref[:, columns] = (rows[:, columns] * scale * gain_ref[:, columns]).astype(BF16)


def shift_pairs(count, stride):
    return [(d, d ^ stride) for d in range(count)]


def entering(state, decay, axis):
    count, place = lax.axis_size(axis), lax.axis_index(axis)
    levels = count.bit_length() - 1
    kept = []
    for level in range(levels - 1):
        stride = 1 << level
        pairs = shift_pairs(count, stride)
        right = ((place >> level) & 1) == 1
        rows = state.shape[0] // 2
        top, bottom = state[:rows], state[rows:]
        mine = jnp.where(right, bottom, top)
        sent = jnp.where(right, top, bottom).astype(BF16)
        got = lax.ppermute(sent, axis, pairs).astype(F32)
        other = lax.ppermute(decay, axis, pairs)
        first, second = jnp.where(right, got, mine), jnp.where(right, mine, got)
        first_decay, second_decay = jnp.where(right, other, decay), jnp.where(right, decay, other)
        kept.append((right, pairs, first, first_decay))
        state, decay = second_decay * first + second, first_decay * second_decay
    stride = count // 2
    prefix = lax.ppermute(state.astype(BF16), axis, [(d, d + stride) for d in range(stride)]).astype(F32)
    for right, pairs, first, first_decay in reversed(kept):
        later = first_decay * prefix + first
        keep = jnp.where(right, later, prefix)
        sent = jnp.where(right, prefix, later).astype(BF16)
        got = lax.ppermute(sent, axis, pairs).astype(F32)
        prefix = jnp.concatenate([jnp.where(right, got, keep), jnp.where(right, keep, got)], axis=0)
    return prefix


def per_device(conv_input, step_raw, conv_weight, conv_bias, step_bias, decay_rate, norm_gain):
    tokens, conv_dim = conv_input.shape
    heads, inner = decay_rate.shape[0], norm_gain.shape[0]
    width = (conv_dim - inner) // 2
    blocks = tokens // GROUP
    count = lax.axis_size("seq")
    before = lax.ppermute(conv_input[tokens - HALO :], "seq", [(d, d + 1) for d in range(count - 1)])
    owner = lax.broadcasted_iota(jnp.int32, (64, inner), 1) // (inner // heads)
    one = (owner == lax.broadcasted_iota(jnp.int32, (64, inner), 0)).astype(BF16)
    spread = jnp.concatenate([one, one], axis=0)

    def whole(*shape):
        return pl.BlockSpec(shape, lambda i: (0, 0))

    def stepped(*shape):
        return pl.BlockSpec(shape, lambda i: (i, 0))

    shape = jax.ShapeDtypeStruct
    xb, bc, a, g, state, decay = pl.pallas_call(
        functools.partial(front_kernel, inner, heads),
        grid=(blocks,),
        in_specs=[
            whole(HALO, conv_dim), stepped(GROUP, conv_dim), stepped(GROUP, heads),
            whole(4, conv_dim), whole(1, conv_dim), whole(1, heads), whole(1, heads),
            whole(128, inner),
        ],
        out_specs=[
            stepped(GROUP, inner), stepped(GROUP, WIDE), stepped(GROUP, 128), stepped(8, inner),
            whole(width, inner), whole(8, inner),
        ],
        out_shape=[
            shape((tokens, inner), BF16), shape((tokens, WIDE), BF16), shape((tokens, 128), BF16),
            shape((8 * blocks, inner), F32), shape((width, inner), F32), shape((8, inner), F32),
        ],
        scratch_shapes=[pltpu.VMEM((HALO + GROUP, conv_dim), F32), pltpu.VMEM((GROUP, 128), F32)],
        name="front",
    )(
        before, conv_input, step_raw, conv_weight, conv_bias[None], step_bias[None],
        decay_rate[None], spread,
    )
    incoming = entering(state, decay[0:1], "seq")
    return pl.pallas_call(
        functools.partial(back_kernel, inner),
        grid=(blocks,),
        in_specs=[
            stepped(GROUP, inner), stepped(GROUP, WIDE), stepped(GROUP, 128), stepped(8, inner),
            whole(128, inner), whole(width, inner), whole(1, inner),
        ],
        out_specs=stepped(GROUP, inner),
        out_shape=shape((tokens, inner), BF16),
        scratch_shapes=[pltpu.VMEM((width, inner), F32), pltpu.VMEM((GROUP, inner), F32)],
        name="back",
    )(xb, bc, a, g, spread, incoming, norm_gain[None])


def solution(mesh):
    placed = (P(("parts", "seq"), None), P(("parts", "seq"), None), P(), P(), P(), P(), P())
    return jax.shard_map(
        per_device, mesh=mesh, in_specs=placed, out_specs=P(("parts", "seq"), None), check_vma=False
    )
```

time: 316 us -> 79.7 us (0.25)
  local copies, waits for them, and re-layouts: 76.6 us -> 6.44 us
  waiting for transfers between devices: 74.8 us -> 18.9 us
  other arithmetic: 60.4 us -> 6.8 us
  matrix products: 49.5 us -> 0 us
  blocking collectives: 35.2 us -> 0 us
  Pallas kernels: 0 us -> 30.5 us
  between operations: 14.3 us -> 0.15 us
  starting transfers between devices: 2.4 us -> 16.4 us
    all_gather x1 -> x0, waiting for transfers between devices: 74.8 us -> none  [entering(): everything = jax.tree.map(lambda part: lax.all_gather(part, axis), array)]
    dot_general x13 -> x0, matrix products: 49.5 us -> none  [the longest x4 22.3 us: block_parts(): jnp.einsum('hts,shp->thp', mixing, values, preferred_element_type=jnp.flo...]
    unnamed x1 -> x0, blocking collectives: 35.2 us -> none
    pallas_call x0 -> x2, Pallas kernels: none -> 30.5 us  [the longest x1 20 us: per_device(): pl.pallas_call(functools.partial(front_kernel, inner, heads), grid=(block...]
    select_n x17 -> x6, other arithmetic: 26.9 us -> 1.39 us  [the longest x3 1.05 us: entering(): jnp.where(right, other, decay)]
    ppermute x1 -> x11, waiting for transfers between devices: 0.01 us -> 18.9 us  [the longest x6 15.6 us: entering(): got = lax.ppermute(sent, axis, pairs).astype(F32)]
    add x1 -> x0, local copies, waits for them, and re-layouts: 17.4 us -> none  [per_device(): return finish(within + across, norm_gain)]
    convert_element_type x2 -> x7, other arithmetic: 16.7 us -> 1.69 us  [the longest x3 1.4 us: entering(): sent = jnp.where(right, top, bottom).astype(BF16)]
  transfers between devices with their start and end apart: 2 -> 11, of which waited for: 1 -> 8; matrix products, arithmetic and copies ran while one was open for 1% -> 10% of each run, Pallas kernels for 0% -> 0%
where the time goes in v1:
time: 79.7 us; the launch traced here: 79.2 us
  Pallas kernels  30.5 us (38%)
  waiting for transfers between devices  18.9 us (24%)
  starting transfers between devices  16.4 us (21%)
  other arithmetic  6.8 us (9%)
  local copies, waits for them, and re-layouts  6.44 us (8%)
    pallas_call x1, Pallas kernels, per_device(): pl.pallas_call(functools.partial(front_kernel, inner, heads), grid=(block...  20 us
    ppermute x6, waiting for transfers between devices, entering(): got = lax.ppermute(sent, axis, pairs).astype(F32)  15.6 us
    pallas_call x1, Pallas kernels, per_device(): pl.pallas_call(functools.partial(back_kernel, inner), grid=(blocks,), in_...  10.5 us
    ppermute x6, starting transfers between devices, entering(): got = lax.ppermute(sent, axis, pairs).astype(F32)  6.28 us
    ppermute x1, starting transfers between devices, entering(): lax.ppermute(state.astype(BF16), axis, [(d, d + stride) for d in range(st...  4.5 us
    ppermute x3, starting transfers between devices, entering(): other = lax.ppermute(decay, axis, pairs)  3.24 us
    unnamed x5, local copies, waits for them, and re-layouts  2.83 us
    ppermute x1, starting transfers between devices, per_device(): lax.ppermute(conv_input[tokens - HALO:], 'seq', [(d, d + 1) for d in rang...  2.39 us
  transfers between devices with their start and end apart: 11, of which 8 were waited for; matrix products, arithmetic and copies ran while one was open for 10% of the time, Pallas kernels for 0%

profile of v1, /device:TPU:0, one launch (start us, length us, event | category | flops | bytes accessed | tf_op | source)
XLA Modules:
  0.0 79.2 jit_solution(5014355332738584191)
XLA Ops:
  0.0 0.8 slice.24
  0.8 2.4 %collective-permute-start = (bf16[8,2816]{1,0:T(8,128)(2,1)S(1)}, bf16[8,2816]{1,0:T(8,128)(2,1)S(1)}, u32[]{:S(2)}, u32[]{:S(2)}) collective-permute-start(bf16[8,2816]{1,0:T(8,128)(2,1)S(1)} %slice.24), channel_id=1, source_target_pairs={{0,1},{1,2},{2,3},{3,4},{4,5},{5,6},{6,7},{7,8},{8,9},{9,10},{10,1... | collective-permute-start | bytes 135176 | tf_op jit(solution)/shard_map/ppermute | solution.py:174
  3.3 0.9 %add_convert_fusion.spread_ref = bf16[128,2560]{1,0:T(8,128)(2,1)} fusion(pred[64,2560]{1,0:T(8,128)(4,1)S(1)} %iota_compare_fusion), kind=kLoop, calls=%fused_computation.1 | loop fusion | flops 655360 | bytes 819200 | tf_op jit(solution)/shard_map/concatenate | solution.py:177
  4.2 1.3 %broadcast_in_dim.12.bias_ref = f32[1,2816]{1,0:T(1,128)} reshape(f32[2816]{0:T(1024)} %param.10) | data formatting | bytes 22528 | tf_op jit(solution)/shard_map/broadcast_in_dim | solution.py:205
  5.5 1.7 %copy.8.raw_ref = bf16[1024,40]{1,0:T(8,128)(2,1)} copy(bf16[1024,40]{0,1:T(8,128)(2,1)} %param.8) | data formatting | bytes 163840 | tf_op args[1]
  7.9 20.0 %front.1 = (bf16[1024,2560]{1,0:T(8,128)(2,1)}, bf16[1024,256]{1,0:T(8,128)(2,1)}, bf16[1024,128]{1,0:T(8,128)(2,1)}, f32[32,2560]{1,0:T(8,128)}, f32[128,2560]{1,0:T(8,128)}, /*index=5*/f32[8,2560]{1,0:T(8,128)}) custom-call(bf16[8,2816]{1,0:T(8,128)(2,1)} %copy-done, bf16[1024,2816]{1,0:T(8,128)(2,1)} %input_ref.1, bf16[1024,40]{1,0:T(8,128)(2,1)} %copy.8.raw_ref, ...), custom_call_target="tpu_custom_call" | custom-call | tf_op jit(solution)/shard_map/front/pallas_call | solution.py:186
  27.9 1.3 %select_convert_fusion.1 = bf16[64,2560]{1,0:T(8,128)(2,1)S(1)} fusion(f32[128,2560]{1,0:T(8,128)} %get-tuple-element.16, pred[]{:T(512)S(6)} %eq.15), kind=kLoop, calls=%fused_computation.11 | loop fusion | flops 163840 | bytes 983041 | tf_op jit(solution)/shard_map/convert_element_type | solution.py:150
  29.2 2.7 %collective-permute-start.4 = (bf16[64,2560]{1,0:T(8,128)(2,1)S(1)}, bf16[64,2560]{1,0:T(8,128)(2,1)S(1)}, u32[]{:S(2)}, u32[]{:S(2)}) collective-permute-start(bf16[64,2560]{1,0:T(8,128)(2,1)S(1)} %select_convert_fusion.1), channel_id=1, source_target_pairs={{0,1},{1,0},{2,3},{3,2},{4,5},{5,4},{6,7},{7,6},{8,9},{9,8},{10,11... | collective-permute-start | bytes 983048 | tf_op jit(solution)/shard_map/ppermute | solution.py:151
  31.9 0.9 %slice.25 = f32[1,2560]{1,0:T(1,128)S(1)} slice(f32[8,2560]{1,0:T(8,128)} %get-tuple-element.15), slice={[0:1], [0:2560]} | slice | bytes 20480 | tf_op jit(solution)/shard_map/slice | solution.py:208
  32.8 1.2 %collective-permute-done.1 = f32[1,2560]{1,0:T(1,128)S(1)} collective-permute-done((f32[1,2560]{1,0:T(1,128)S(1)}, f32[1,2560]{1,0:T(1,128)S(1)}, u32[]{:S(2)}, u32[]{:S(2)}) %collective-permute-start.1) | collective-permute-done | bytes 10272 | tf_op jit(solution)/shard_map/ppermute | solution.py:152
  34.0 0.9 %fusion.16 = (f32[2560]{0:T(1024)S(1)}, f32[2560]{0:T(1024)S(1)}, f32[1,2560]{1,0:T(1,128)S(1)}) fusion(f32[1,2560]{1,0:T(1,128)S(1)} %collective-permute-done.1, pred[]{:T(512)S(6)} %eq.15, f32[8,2560]{1,0:T(8,128)} %get-tuple-element.15), kind=kLoop, calls=%fused_computation.56 | loop fusion | flops 7680 | bytes 51201 | tf_op jit(solution)/shard_map/jit(_where)/select_n | solution.py:154
  34.9 1.6 %collective-permute-start.2 = (f32[1,2560]{1,0:T(1,128)S(1)}, f32[1,2560]{1,0:T(1,128)S(1)}, u32[]{:S(2)}, u32[]{:S(2)}) collective-permute-start(f32[1,2560]{1,0:T(1,128)S(1)} %get-tuple-element.35), channel_id=1, source_target_pairs={{0,2},{1,3},{2,0},{3,1},{4,6},{5,7},{6,4},{7,5},{8,10},{9,11},{10,... | collective-permute-start | bytes 30728 | tf_op jit(solution)/shard_map/ppermute | solution.py:152
  36.5 1.4 %fusion = (f32[64,2560]{1,0:T(8,128)S(1)}, f32[64,2560]{1,0:T(8,128)S(1)}) fusion(bf16[64,2560]{1,0:T(8,128)(2,1)S(1)} %collective-permute-done.4, f32[2560]{0:T(1024)S(1)} %get-tuple-element.18, pred[]{:T(512)S(6)} %eq.15, f32[128,2560]{1,0:T(8,128)} %get-tuple-element.16), kind=kLoop, calls=%fused_computation.6 | loop fusion | flops 983040 | bytes 2959361 | tf_op jit(solution)/shard_map/add | solution.py:156
  38.7 1.6 %collective-permute-start.3 = (f32[1,2560]{1,0:T(1,128)S(1)}, f32[1,2560]{1,0:T(1,128)S(1)}, u32[]{:S(2)}, u32[]{:S(2)}) collective-permute-start(f32[1,2560]{1,0:T(1,128)S(1)} %get-tuple-element.36), channel_id=1, source_target_pairs={{0,4},{1,5},{2,6},{3,7},{4,0},{5,1},{6,2},{7,3},{8,12},{9,13},{10,... | collective-permute-start | bytes 30728 | tf_op jit(solution)/shard_map/ppermute | solution.py:152
  40.4 3.7 %collective-permute-done.5 = bf16[32,2560]{1,0:T(8,128)(2,1)S(1)} collective-permute-done((bf16[32,2560]{1,0:T(8,128)(2,1)S(1)}, bf16[32,2560]{1,0:T(8,128)(2,1)S(1)}, u32[]{:S(2)}, u32[]{:S(2)}) %collective-permute-start.5) | collective-permute-done | bytes 163872 | tf_op jit(solution)/shard_map/ppermute | solution.py:151
  44.1 1.6 %collective-permute-start.6 = (bf16[16,2560]{1,0:T(8,128)(2,1)S(1)}, bf16[16,2560]{1,0:T(8,128)(2,1)S(1)}, u32[]{:S(2)}, u32[]{:S(2)}) collective-permute-start(bf16[16,2560]{1,0:T(8,128)(2,1)S(1)} %select_convert_fusion.4), channel_id=1, source_target_pairs={{0,4},{1,5},{2,6},{3,7},{4,0},{5,1},{6,2},{7,3},{8,12},{9,13},{10,... | collective-permute-start | bytes 245768 | tf_op jit(solution)/shard_map/ppermute | solution.py:151
  45.8 2.8 %collective-permute-done.6 = bf16[16,2560]{1,0:T(8,128)(2,1)S(1)} collective-permute-done((bf16[16,2560]{1,0:T(8,128)(2,1)S(1)}, bf16[16,2560]{1,0:T(8,128)(2,1)S(1)}, u32[]{:S(2)}, u32[]{:S(2)}) %collective-permute-start.6) | collective-permute-done | bytes 81952 | tf_op jit(solution)/shard_map/ppermute | solution.py:151
  48.7 4.5 %collective-permute-start.7 = (bf16[16,2560]{1,0:T(8,128)(2,1)S(1)}, bf16[16,2560]{1,0:T(8,128)(2,1)S(1)}, u32[]{:S(2)}, u32[]{:S(2)}) collective-permute-start(bf16[16,2560]{1,0:T(8,128)(2,1)S(1)} %get-tuple-element.23), channel_id=1, source_target_pairs={{0,8},{1,9},{2,10},{3,11},{4,12},{5,13},{6,14},{7,15},{16,24},{17,... | collective-permute-start | bytes 245768 | tf_op jit(solution)/shard_map/ppermute | solution.py:158
  53.2 2.0 %collective-permute-done.7 = bf16[16,2560]{1,0:T(8,128)(2,1)S(1)} collective-permute-done((bf16[16,2560]{1,0:T(8,128)(2,1)S(1)}, bf16[16,2560]{1,0:T(8,128)(2,1)S(1)}, u32[]{:S(2)}, u32[]{:S(2)}) %collective-permute-start.7) | collective-permute-done | bytes 81952 | tf_op jit(solution)/shard_map/ppermute | solution.py:158
  55.7 4.1 %collective-permute-done.8 = bf16[16,2560]{1,0:T(8,128)(2,1)S(1)} collective-permute-done((bf16[16,2560]{1,0:T(8,128)(2,1)S(1)}, bf16[16,2560]{1,0:T(8,128)(2,1)S(1)}, u32[]{:S(2)}, u32[]{:S(2)}) %collective-permute-start.8) | collective-permute-done | bytes 81952 | tf_op jit(solution)/shard_map/ppermute | solution.py:163
  59.9 0.9 %collective-permute-start.9 = (bf16[32,2560]{1,0:T(8,128)(2,1)S(1)}, bf16[32,2560]{1,0:T(8,128)(2,1)S(1)}, u32[]{:S(2)}, u32[]{:S(2)}) collective-permute-start(bf16[32,2560]{1,0:T(8,128)(2,1)S(1)} %select_convert_fusion.2), channel_id=1, source_target_pairs={{0,2},{1,3},{2,0},{3,1},{4,6},{5,7},{6,4},{7,5},{8,10},{9,11},{10,... | collective-permute-start | bytes 491528 | tf_op jit(solution)/shard_map/ppermute | solution.py:163
  60.8 4.5 %collective-permute-done.9 = bf16[32,2560]{1,0:T(8,128)(2,1)S(1)} collective-permute-done((bf16[32,2560]{1,0:T(8,128)(2,1)S(1)}, bf16[32,2560]{1,0:T(8,128)(2,1)S(1)}, u32[]{:S(2)}, u32[]{:S(2)}) %collective-permute-start.9) | collective-permute-done | bytes 163872 | tf_op jit(solution)/shard_map/ppermute | solution.py:163
  67.5 1.2 %pad_maximum_fusion.incoming_ref = f32[128,2560]{1,0:T(8,128)} fusion(f32[64,2560]{1,0:T(8,128)S(1)} %get-tuple-element.30, f32[64,2560]{1,0:T(8,128)S(1)} %get-tuple-element.29), kind=kLoop, calls=%fused_computation | loop fusion | flops 327680 | bytes 2621440 | tf_op jit(solution)/shard_map/concatenate | solution.py:164
  68.6 10.5 %back.1 = bf16[1024,2560]{1,0:T(8,128)(2,1)} custom-call(bf16[1024,2560]{1,0:T(8,128)(2,1)} %get-tuple-element.11.xb_ref, bf16[1024,256]{1,0:T(8,128)(2,1)} %get-tuple-element.12.bc_ref, bf16[1024,128]{1,0:T(8,128)(2,1)} %get-tuple-element.13.a_ref, f32[32,2560]{1,0:T(8,128)} %get-tuple-element.14.g_ref, bf16[128,2560]{1,0:T(8,128)(2,1)} %add_convert_fusion.spread_ref, ...), custom_call_target="tpu_custom_call" | custom-call | tf_op jit(solution)/shard_map/back/pallas_call | solution.py:209
  (29 shorter events, 4.4 us)
Async XLA Ops:
  0.8 6.5 %collective-permute-start = (bf16[8,2816]{1,0:T(8,128)(2,1)S(1)}, bf16[8,2816]{1,0:T(8,128)(2,1)S(1)}, u32[]{:S(2)}, u32[]{:S(2)}) collective-permute-start(bf16[8,2816]{1,0:T(8,128)(2,1)S(1)} %slice.24), channel_id=1, source_target_pairs={{0,1},{1,2},{2,3},{3,4},{4,5},{5,6},{6,7},{7,8},{8,9},{9,10},{10,1... | collective-permute-start | bytes 135176 | tf_op jit(solution)/shard_map/ppermute | solution.py:174
  7.3 0.6 copy-start
  29.2 7.3 %collective-permute-start.4 = (bf16[64,2560]{1,0:T(8,128)(2,1)S(1)}, bf16[64,2560]{1,0:T(8,128)(2,1)S(1)}, u32[]{:S(2)}, u32[]{:S(2)}) collective-permute-start(bf16[64,2560]{1,0:T(8,128)(2,1)S(1)} %select_convert_fusion.1), channel_id=1, source_target_pairs={{0,1},{1,0},{2,3},{3,2},{4,5},{5,4},{6,7},{7,6},{8,9},{9,8},{10,11... | collective-permute-start | bytes 983048 | tf_op jit(solution)/shard_map/ppermute | solution.py:151
  32.8 1.2 %collective-permute-start.1 = (f32[1,2560]{1,0:T(1,128)S(1)}, f32[1,2560]{1,0:T(1,128)S(1)}, u32[]{:S(2)}, u32[]{:S(2)}) collective-permute-start(f32[1,2560]{1,0:T(1,128)S(1)} %slice.25), channel_id=1, source_target_pairs={{0,1},{1,0},{2,3},{3,2},{4,5},{5,4},{6,7},{7,6},{8,9},{9,8},{10,11... | collective-permute-start | bytes 30728 | tf_op jit(solution)/shard_map/ppermute | solution.py:152
  34.9 3.7 %collective-permute-start.2 = (f32[1,2560]{1,0:T(1,128)S(1)}, f32[1,2560]{1,0:T(1,128)S(1)}, u32[]{:S(2)}, u32[]{:S(2)}) collective-permute-start(f32[1,2560]{1,0:T(1,128)S(1)} %get-tuple-element.35), channel_id=1, source_target_pairs={{0,2},{1,3},{2,0},{3,1},{4,6},{5,7},{6,4},{7,5},{8,10},{9,11},{10,... | collective-permute-start | bytes 30728 | tf_op jit(solution)/shard_map/ppermute | solution.py:152
  38.0 6.1 %collective-permute-start.5 = (bf16[32,2560]{1,0:T(8,128)(2,1)S(1)}, bf16[32,2560]{1,0:T(8,128)(2,1)S(1)}, u32[]{:S(2)}, u32[]{:S(2)}) collective-permute-start(bf16[32,2560]{1,0:T(8,128)(2,1)S(1)} %select_convert_fusion.3), channel_id=1, source_target_pairs={{0,2},{1,3},{2,0},{3,1},{4,6},{5,7},{6,4},{7,5},{8,10},{9,11},{10,... | collective-permute-start | bytes 491528 | tf_op jit(solution)/shard_map/ppermute | solution.py:151
  38.7 7.1 %collective-permute-start.3 = (f32[1,2560]{1,0:T(1,128)S(1)}, f32[1,2560]{1,0:T(1,128)S(1)}, u32[]{:S(2)}, u32[]{:S(2)}) collective-permute-start(f32[1,2560]{1,0:T(1,128)S(1)} %get-tuple-element.36), channel_id=1, source_target_pairs={{0,4},{1,5},{2,6},{3,7},{4,0},{5,1},{6,2},{7,3},{8,12},{9,13},{10,... | collective-permute-start | bytes 30728 | tf_op jit(solution)/shard_map/ppermute | solution.py:152
  44.1 4.5 %collective-permute-start.6 = (bf16[16,2560]{1,0:T(8,128)(2,1)S(1)}, bf16[16,2560]{1,0:T(8,128)(2,1)S(1)}, u32[]{:S(2)}, u32[]{:S(2)}) collective-permute-start(bf16[16,2560]{1,0:T(8,128)(2,1)S(1)} %select_convert_fusion.4), channel_id=1, source_target_pairs={{0,4},{1,5},{2,6},{3,7},{4,0},{5,1},{6,2},{7,3},{8,12},{9,13},{10,... | collective-permute-start | bytes 245768 | tf_op jit(solution)/shard_map/ppermute | solution.py:151
  48.7 6.5 %collective-permute-start.7 = (bf16[16,2560]{1,0:T(8,128)(2,1)S(1)}, bf16[16,2560]{1,0:T(8,128)(2,1)S(1)}, u32[]{:S(2)}, u32[]{:S(2)}) collective-permute-start(bf16[16,2560]{1,0:T(8,128)(2,1)S(1)} %get-tuple-element.23), channel_id=1, source_target_pairs={{0,8},{1,9},{2,10},{3,11},{4,12},{5,13},{6,14},{7,15},{16,24},{17,... | collective-permute-start | bytes 245768 | tf_op jit(solution)/shard_map/ppermute | solution.py:158
  55.3 4.5 %collective-permute-start.8 = (bf16[16,2560]{1,0:T(8,128)(2,1)S(1)}, bf16[16,2560]{1,0:T(8,128)(2,1)S(1)}, u32[]{:S(2)}, u32[]{:S(2)}) collective-permute-start(bf16[16,2560]{1,0:T(8,128)(2,1)S(1)} %fusion.7), channel_id=1, source_target_pairs={{0,4},{1,5},{2,6},{3,7},{4,0},{5,1},{6,2},{7,3},{8,12},{9,13},{10,... | collective-permute-start | bytes 245768 | tf_op jit(solution)/shard_map/ppermute | solution.py:163
  59.9 5.4 %collective-permute-start.9 = (bf16[32,2560]{1,0:T(8,128)(2,1)S(1)}, bf16[32,2560]{1,0:T(8,128)(2,1)S(1)}, u32[]{:S(2)}, u32[]{:S(2)}) collective-permute-start(bf16[32,2560]{1,0:T(8,128)(2,1)S(1)} %select_convert_fusion.2), channel_id=1, source_target_pairs={{0,2},{1,3},{2,0},{3,1},{4,6},{5,7},{6,4},{7,5},{8,10},{9,11},{10,... | collective-permute-start | bytes 491528 | tf_op jit(solution)/shard_map/ppermute | solution.py:163
  65.4 0.7 copy-start.1
  65.6 1.7 %collective-permute-start.10 = (bf16[64,2560]{1,0:T(8,128)(2,1)S(1)}, bf16[64,2560]{1,0:T(8,128)(2,1)S(1)}, u32[]{:S(2)}, u32[]{:S(2)}) collective-permute-start(bf16[64,2560]{1,0:T(8,128)(2,1)S(1)} %select_convert_fusion), channel_id=1, source_target_pairs={{0,1},{1,0},{2,3},{3,2},{4,5},{5,4},{6,7},{7,6},{8,9},{9,8},{10,11... | collective-permute-start | bytes 983048 | tf_op jit(solution)/shard_map/ppermute | solution.py:163

commit v2 on v1

v2 whole, which is shorter than its diff:
```python
import functools

import jax
import jax.numpy as jnp
from jax import lax
from jax.experimental import pallas as pl
from jax.experimental.pallas import tpu as pltpu
from jax.sharding import PartitionSpec as P

GROUP = 256
WIDE = 256
LANES = 128
PARTS = 2
HALO = 8
F32, BF16 = jnp.float32, jnp.bfloat16


def dot(left, right):
    return jnp.dot(left, right, preferred_element_type=F32)


def split(value):
    high = value.astype(BF16).astype(F32)
    return high, value - high


def lower_triangle():
    rows = lax.broadcasted_iota(jnp.int32, (GROUP, GROUP), 0)
    columns = lax.broadcasted_iota(jnp.int32, (GROUP, GROUP), 1)
    return rows >= columns


def fill_spread(spread, heads):
    width = spread.shape[1] // heads
    rows = lax.broadcasted_iota(jnp.int32, spread.shape, 0)
    columns = lax.broadcasted_iota(jnp.int32, spread.shape, 1)
    rows = jnp.where(rows >= LANES // 2, rows - LANES // 2, rows)
    start = rows * width
    spread[...] = jnp.where((columns >= start) & (columns < start + width), 1.0, 0.0).astype(BF16)


def front_kernel(
    inner, heads, blocks, count,
    before_ref, input_ref, whole_ref, raw_ref, weight_ref, bias_ref, step_bias_ref, rate_ref,
    xb_ref, bc_ref, a_ref, g_ref, state_ref,
    buf, halo, spread, pack, square, b_packs, g_packs, log_send, log_recv, log_first, log_second, wide_decay,
    keep, down_send, down_recv, top_send, top_recv, up_send, up_recv,
    halo_sems, log_sems, down_sems, top_sems, up_sems,
):
    at = pl.program_id(0)
    place = lax.axis_index("seq")
    levels = count.bit_length() - 1
    halvings = levels - 1
    half = LANES // 2
    tokens = blocks * GROUP
    rights = [lax.rem(place // (1 << level), 2) for level in range(levels)]
    partners = [place + (1 << level) * (1 - 2 * rights[level]) for level in range(levels)]
    behind, ahead = lax.rem(place + count - 1, count), lax.rem(place + 1, count)

    def send(source, target, sems, device):
        return pltpu.make_async_remote_copy(
            src_ref=source, dst_ref=target, send_sem=sems.at[0], recv_sem=sems.at[1],
            device_id={"seq": device}, device_id_type=pl.DeviceIdType.MESH,
        )

    halo_copy = send(whole_ref.at[pl.ds(tokens - 16, 16)], halo, halo_sems, ahead)

    def log_copy(level):
        return send(log_send.at[level], log_recv.at[level], log_sems.at[level], partners[level])

    def log_finish(level):
        log_copy(level).wait()
        own, other = log_send[level], log_recv[level]
        log_first[level] = jnp.where(rights[level] == 1, other, own)
        log_second[level] = jnp.where(rights[level] == 1, own, other)
        if level + 1 < halvings:
            log_send[level + 1] = own + other
            log_copy(level + 1).start()

    def turned(high, low):
        square[0:heads] = jnp.broadcast_to(high, (heads, LANES))
        square[half : half + heads] = jnp.broadcast_to(low, (heads, LANES))
        return square[...].T[0:8]

    def column(ref):
        square[0:1, 0:heads] = ref[...].reshape(1, heads)
        return jnp.broadcast_to(square[0:1], (LANES, LANES)).T[0:heads, 0:1]

    @pl.when(at == 0)
    def _():
        barrier = pltpu.get_barrier_semaphore()
        for device in partners + [behind, ahead]:
            pl.semaphore_signal(barrier, inc=1, device_id={"seq": device}, device_id_type=pl.DeviceIdType.MESH)
        square[...] = jnp.zeros_like(square)
        pack[...] = jnp.zeros_like(pack)
        step_bias, rate = column(step_bias_ref), column(rate_ref)
        square[...] = jnp.zeros_like(square)
        shifted = raw_ref[...].astype(F32) + step_bias
        step = jnp.maximum(shifted, 0.0) + jnp.log(1.0 + jnp.exp(-jnp.abs(shifted)))
        logs = -rate * step
        total = jnp.sum(logs, axis=1, keepdims=True)
        log_send[0] = turned(total, jnp.zeros_like(total))
        pl.semaphore_wait(barrier, levels + 2)
        if halvings > 0:
            log_copy(0).start()
        halo_copy.start()
        fill_spread(spread, heads)
        state_ref[...] = jnp.zeros_like(state_ref)
        ones = lower_triangle().astype(F32).T.astype(BF16)
        high, rest = split(logs)
        middle, low = split(rest)
        for block in range(blocks):
            span = slice(block * GROUP, (block + 1) * GROUP)
            cum = dot(high[:, span].astype(BF16), ones) + (
                dot(middle[:, span].astype(BF16), ones) + dot(low[:, span].astype(BF16), ones)
            )
            mid = 0.5 * cum[:, GROUP - 1 : GROUP]
            first, second = split(jnp.exp(cum - mid))
            pack[0:heads, :] = first
            pack[half : half + heads, :] = second
            a_ref[span] = pack[...].T.astype(BF16)
            first, second = split(jnp.exp(mid - cum) * step[:, span])
            pack[0:heads, :] = first
            pack[half : half + heads, :] = second
            b_packs[span] = pack[...].T.astype(BF16)
            first, second = split(jnp.exp(mid))
            g_packs[8 * block : 8 * block + 8] = turned(first, second)

    @pl.when(at < blocks - 1)
    def _():
        buf[0:HALO] = before_ref[HALO : 2 * HALO].astype(F32)

    for level in range(min(halvings, blocks - 2)):
        @pl.when(at == level + 1)
        def _():
            log_finish(level)

    last = at == blocks - 1

    @pl.when(last)
    def _():
        for level in range(min(halvings, blocks - 2), halvings):
            log_finish(level)
        halo_copy.wait()
        buf[0:HALO] = jnp.where(place == 0, 0.0, halo[HALO : 2 * HALO].astype(F32))

    block = lax.rem(at + 1, blocks)
    b_pack = b_packs[pl.ds(pl.multiple_of(block * GROUP, GROUP), GROUP)]
    g_pack = g_packs[pl.ds(pl.multiple_of(block * 8, 8), 8)].astype(BF16)

    def mix(columns):
        buf[HALO : HALO + GROUP, columns] = input_ref[:, columns].astype(F32)
        total = bias_ref[columns].reshape(1, WIDE) + buf[HALO - 3 : HALO - 3 + GROUP, columns] * weight_ref[0:1, columns]
        for k in range(1, 4):
            total = total + buf[HALO - 3 + k : HALO - 3 + k + GROUP, columns] * weight_ref[k : k + 1, columns]
        part = 0.5 * total
        return (part + part * jnp.tanh(part)).astype(BF16)

    bc = mix(slice(inner, inner + WIDE))
    bc_ref[...] = bc
    b_turned = bc[:, : WIDE // 2].astype(F32).T.astype(BF16)

    def chunk(j):
        columns = slice(j * WIDE, (j + 1) * WIDE)
        wide = spread[:, columns]
        xb = (mix(columns).astype(F32) * dot(b_pack, wide)).astype(BF16)
        xb_ref[:, columns] = xb
        g8 = dot(g_pack, wide)
        g_ref[:, columns] = g8
        return columns, g8[0:1], dot(b_turned, xb)

    @pl.when(at < blocks - 1)
    def _():
        for j in range(inner // WIDE):
            columns, g, update = chunk(j)
            state_ref[:, columns] = g * (g * state_ref[:, columns] + update)
            wide_decay[0:8, columns] = jnp.where(at == 0, 1.0, wide_decay[0:8, columns]) * (g * g)

    group = inner // PARTS

    def part_of(part):
        return slice(part * group, (part + 1) * group)

    def rows_of(level):
        return LANES >> (level + 1)

    def decay_row(level, which, columns):
        row = 8 + 16 * level + 8 * which
        return wide_decay[row : row + 1, columns]

    def down_copy(level, part):
        return send(down_send[level].at[part], down_recv[level].at[part], down_sems.at[level, part], partners[level])

    def up_copy(level, part):
        return send(up_send[level].at[part], up_recv[level].at[part], up_sems.at[level, part], partners[level])

    def top_copy(part):
        return send(top_send.at[part], top_recv.at[part], top_sems.at[part], partners[levels - 1])

    def down_start(level, part):
        if level == halvings:
            top_send[part] = state_ref[0 : LANES >> level, part_of(part)].astype(BF16)
            top_copy(part).start()
            return
        rows, columns, right = rows_of(level), part_of(part), rights[level] == 1
        top, bottom = state_ref[0:rows, columns], state_ref[rows : 2 * rows, columns]
        down_send[level][part] = jnp.where(right, top, bottom).astype(BF16)
        down_copy(level, part).start()
        keep[level][:, columns] = jnp.where(right, bottom, top)

    def down_finish(level, part):
        rows, columns, right = rows_of(level), part_of(part), rights[level] == 1
        down_copy(level, part).wait()
        got, mine = down_recv[level][part].astype(F32), keep[level][:, columns]
        first, second = jnp.where(right, got, mine), jnp.where(right, mine, got)
        state_ref[0:rows, columns] = decay_row(level, 1, columns) * first + second
        keep[level][:, columns] = first

    def up_start(level, part):
        rows, columns, right = rows_of(level), part_of(part), rights[level] == 1
        prefix = state_ref[0:rows, columns]
        later = decay_row(level, 0, columns) * prefix + keep[level][:, columns]
        up_send[level][part] = jnp.where(right, prefix, later).astype(BF16)
        up_copy(level, part).start()
        keep[level][:, columns] = jnp.where(right, later, prefix)

    def up_finish(level, part):
        rows, columns, right = rows_of(level), part_of(part), rights[level] == 1
        up_copy(level, part).wait()
        got, mine = up_recv[level][part].astype(F32), keep[level][:, columns]
        state_ref[0:rows, columns] = jnp.where(right, got, mine)
        state_ref[rows : 2 * rows, columns] = jnp.where(right, mine, got)

    @pl.when(last)
    def _():
        decays = []
        for level in range(halvings):
            for log in (log_first[level], log_second[level]):
                first, second = split(jnp.exp(log))
                lane = lax.broadcasted_iota(jnp.int32, (8, LANES), 1)
                decays.append(jnp.where(lane < half, first, pltpu.roll(second, half, 1)))
        decay_pack = jnp.concatenate(decays, axis=0).astype(BF16)
        for j in range(inner // WIDE):
            columns, g, update = chunk(j)
            state_ref[:, columns] = state_ref[:, columns] + wide_decay[0:1, columns] * (g * update)
            wide_decay[8 : 8 + 16 * halvings, columns] = dot(decay_pack, spread[:, columns])
            for part in range(PARTS):
                if (part + 1) * group == (j + 1) * WIDE:
                    down_start(0, part)
        for level in range(halvings):
            for part in range(PARTS):
                down_finish(level, part)
                down_start(level + 1, part)
        for part in range(PARTS):
            top_copy(part).wait()
            state_ref[0 : LANES >> halvings, part_of(part)] = jnp.where(
                rights[levels - 1] == 1, top_recv[part].astype(F32), 0.0
            )
            up_start(halvings - 1, part)
        for level in reversed(range(halvings)):
            for part in range(PARTS):
                up_finish(level, part)
                if level > 0:
                    up_start(level - 1, part)


def back_kernel(
    inner, heads,
    xb_ref, bc_ref, a_ref, g_ref, incoming_ref, gain_ref,
    out_ref,
    state, rows, spread,
):
    @pl.when(pl.program_id(0) == 0)
    def _():
        state[...] = incoming_ref[...]
        fill_spread(spread, heads)

    bc = bc_ref[...]
    width = WIDE // 2
    b, c = bc[:, :width], bc[:, width:]
    b_turned = b.astype(F32).T.astype(BF16)
    scores = dot(c, b_turned)
    scores = jnp.where(lower_triangle(), scores, 0.0).astype(BF16)
    c_twice = jnp.concatenate([c, c], axis=1)
    a_pack = a_ref[...]
    squares = jnp.zeros((GROUP, WIDE), F32)
    for j in range(inner // WIDE):
        columns = slice(j * WIDE, (j + 1) * WIDE)
        xb = xb_ref[:, columns]
        g = g_ref[0:1, columns]
        held = g * state[:, columns]
        high = held.astype(BF16)
        low = (held - high.astype(F32)).astype(BF16)
        total = dot(scores, xb) + dot(c_twice, jnp.concatenate([high, low], axis=0))
        y = total * dot(a_pack, spread[:, columns])
        rows[:, columns] = y
        squares = squares + y * y
        state[:, columns] = g * (held + dot(b_turned, xb))
    mean = jnp.sum(squares, axis=1, keepdims=True) * (1.0 / inner)
    scale = lax.rsqrt(mean + 1e-05)
    for j in range(inner // WIDE):
        columns = slice(j * WIDE, (j + 1) * WIDE)
        out_ref[:, columns] = (rows[:, columns] * scale * gain_ref[columns].reshape(1, WIDE)).astype(BF16)


def per_device(conv_input, step_raw, conv_weight, conv_bias, step_bias, decay_rate, norm_gain):
    tokens, conv_dim = conv_input.shape
    heads, inner = decay_rate.shape[0], norm_gain.shape[0]
    blocks = tokens // GROUP
    count = lax.axis_size("seq")
    levels = count.bit_length() - 1
    halvings = levels - 1
    group = inner // PARTS
    sizes = [LANES >> (level + 1) for level in range(halvings)]

    def whole(*shape):
        return pl.BlockSpec(shape, lambda i: (0,) * len(shape))

    def stepped(*shape):
        return pl.BlockSpec(shape, lambda i: (i, 0))

    def turned(*shape):
        return pl.BlockSpec(shape, lambda i: (lax.rem(i + 1, blocks), 0))

    def vmem(*shape, dtype=F32):
        return pltpu.VMEM(shape, dtype)

    slots = [vmem(PARTS, rows, group, dtype=BF16) for rows in sizes]
    shape = jax.ShapeDtypeStruct
    xb, bc, a, g, state = pl.pallas_call(
        functools.partial(front_kernel, inner, heads, blocks, count),
        grid=(blocks,),
        in_specs=[
            pl.BlockSpec((16, conv_dim), lambda i: (jnp.maximum(lax.rem(i + 1, blocks) * (GROUP // 16) - 1, 0), 0)),
            turned(GROUP, conv_dim), pl.BlockSpec(memory_space=pl.ANY),
            whole(heads, tokens), whole(4, conv_dim), whole(conv_dim), whole(heads), whole(heads),
        ],
        out_specs=[
            turned(GROUP, inner), turned(GROUP, WIDE), whole(tokens, LANES), turned(8, inner),
            whole(LANES, inner),
        ],
        out_shape=[
            shape((tokens, inner), BF16), shape((tokens, WIDE), BF16), shape((tokens, LANES), BF16),
            shape((8 * blocks, inner), F32), shape((LANES, inner), F32),
        ],
        scratch_shapes=[
            vmem(HALO + GROUP, conv_dim), vmem(16, conv_dim, dtype=BF16), vmem(LANES, inner, dtype=BF16),
            vmem(LANES, GROUP), vmem(LANES, LANES), vmem(tokens, LANES, dtype=BF16), vmem(8 * blocks, LANES),
            vmem(halvings, 8, LANES), vmem(halvings, 8, LANES), vmem(halvings, 8, LANES), vmem(halvings, 8, LANES),
            vmem(8 + 16 * halvings, inner),
            [vmem(rows, inner) for rows in sizes], slots, slots,
            vmem(PARTS, LANES >> halvings, group, dtype=BF16), vmem(PARTS, LANES >> halvings, group, dtype=BF16),
            slots, slots,
            pltpu.SemaphoreType.DMA((2,)), pltpu.SemaphoreType.DMA((halvings, 2)),
            pltpu.SemaphoreType.DMA((halvings, PARTS, 2)), pltpu.SemaphoreType.DMA((PARTS, 2)),
            pltpu.SemaphoreType.DMA((halvings, PARTS, 2)),
        ],
        compiler_params=pltpu.CompilerParams(collective_id=0, has_side_effects=True, vmem_limit_bytes=60 * 1024 * 1024),
        name="front",
    )(conv_input, conv_input, conv_input, step_raw.T, conv_weight, conv_bias, step_bias, decay_rate)
    return pl.pallas_call(
        functools.partial(back_kernel, inner, heads),
        grid=(blocks,),
        in_specs=[
            stepped(GROUP, inner), stepped(GROUP, WIDE), stepped(GROUP, LANES), stepped(8, inner),
            whole(LANES, inner), whole(inner),
        ],
        out_specs=stepped(GROUP, inner),
        out_shape=shape((tokens, inner), BF16),
        scratch_shapes=[vmem(LANES, inner), vmem(GROUP, inner), vmem(LANES, inner, dtype=BF16)],
        name="back",
    )(xb, bc, a, g, state, norm_gain)


def solution(mesh):
    placed = (P(("parts", "seq"), None), P(("parts", "seq"), None), P(), P(), P(), P(), P())
    return jax.shard_map(
        per_device, mesh=mesh, in_specs=placed, out_specs=P(("parts", "seq"), None), check_vma=False
    )
```

time: 79.7 us -> 55.6 us (0.70)
  Pallas kernels: 30.5 us -> 55.4 us
  waiting for transfers between devices: 18.9 us -> 0 us
  starting transfers between devices: 16.4 us -> 0 us
  other arithmetic: 6.8 us -> 0 us
  local copies, waits for them, and re-layouts: 6.44 us -> 0 us
    pallas_call x2, Pallas kernels: 30.5 us -> 55.4 us  [the longest x1 44.9 us: per_device(): pl.pallas_call(functools.partial(front_kernel, inner, heads, blocks, coun...]
    ppermute x11 -> x0, waiting for transfers between devices: 18.9 us -> none  [the longest x6 15.6 us: entering(): got = lax.ppermute(sent, axis, pairs).astype(F32)]
    ppermute x11 -> x0, starting transfers between devices: 16.4 us -> none  [the longest x6 6.28 us: entering(): got = lax.ppermute(sent, axis, pairs).astype(F32)]
    unnamed x5 -> x0, local copies, waits for them, and re-layouts: 2.83 us -> none
    concatenate x2 -> x0, other arithmetic: 2.1 us -> none  [the longest x1 1.2 us: entering(): jnp.concatenate([jnp.where(right, got, keep), jnp.where(right, keep, got)...]
    broadcast_in_dim x2 -> x0, local copies, waits for them, and re-layouts: 1.93 us -> none  [the longest x1 1.31 us: per_device(): conv_bias[None]]
    convert_element_type x7 -> x0, other arithmetic: 1.69 us -> none  [the longest x3 1.4 us: entering(): sent = jnp.where(right, top, bottom).astype(BF16)]
    slice x2 -> x0, local copies, waits for them, and re-layouts: 1.68 us -> none  [the longest x1 0.89 us: per_device(): incoming = entering(state, decay[0:1], 'seq')]
  transfers between devices with their start and end apart: 11 -> 0, of which waited for: 8 -> 0; matrix products, arithmetic and copies ran while one was open for 10% -> 0% of each run, Pallas kernels for 0% -> 0%
where the time goes in v2:
time: 55.6 us; the launch traced here: 55.4 us
  Pallas kernels  55.4 us (100%)
    pallas_call x1, Pallas kernels, per_device(): pl.pallas_call(functools.partial(front_kernel, inner, heads, blocks, coun...  44.9 us
    pallas_call x1, Pallas kernels, per_device(): pl.pallas_call(functools.partial(back_kernel, inner, heads), grid=(blocks...  10.5 us

profile of v2, /device:TPU:0, one launch (start us, length us, event | category | flops | bytes accessed | tf_op | source)
XLA Modules:
  0.0 55.4 jit_solution(7833196955358050092)
XLA Ops:
  0.0 44.9 %front.1 = (bf16[1024,2560]{1,0:T(8,128)(2,1)}, bf16[1024,256]{1,0:T(8,128)(2,1)}, bf16[1024,128]{1,0:T(8,128)(2,1)}, f32[32,2560]{1,0:T(8,128)}, f32[128,2560]{1,0:T(8,128)}) custom-call(bf16[1024,2816]{1,0:T(8,128)(2,1)} %whole_ref.1, bf16[1024,2816]{1,0:T(8,128)(2,1)} %whole_ref.1, bf16[1024,2816]{1,0:T(8,128)(2,1)} %whole_ref.1, ...), custom_call_target="tpu_custom_call" | custom-call | tf_op jit(solution)/shard_map/front/pallas_call | solution.py:330
  44.9 10.5 %back.1 = bf16[1024,2560]{1,0:T(8,128)(2,1)} custom-call(bf16[1024,2560]{1,0:T(8,128)(2,1)} %get-tuple-element.10.xb_ref, bf16[1024,256]{1,0:T(8,128)(2,1)} %get-tuple-element.11.bc_ref, bf16[1024,128]{1,0:T(8,128)(2,1)} %get-tuple-element.12.a_ref, f32[32,2560]{1,0:T(8,128)} %get-tuple-element.13.g_ref, f32[128,2560]{1,0:T(8,128)} %get-tuple-element.14.incoming_ref, ...), custom_call_target="tpu_custom_call" | custom-call | tf_op jit(solution)/shard_map/back/pallas_call | solution.py:361

commit v3 on v2

--- a/solution.py
+++ b/solution.py
@@ -10,7 +10,7 @@
 GROUP = 256
 WIDE = 256
 LANES = 128
-PARTS = 2
+PARTS = 5
 HALO = 8
 F32, BF16 = jnp.float32, jnp.bfloat16
 
@@ -41,9 +41,9 @@
 
 def front_kernel(
     inner, heads, blocks, count,
-    before_ref, input_ref, whole_ref, raw_ref, weight_ref, bias_ref, step_bias_ref, rate_ref,
+    input_ref, bc_in_ref, whole_ref, raw_ref, weight_ref, bias_ref, step_bias_ref, rate_ref,
     xb_ref, bc_ref, a_ref, g_ref, state_ref,
-    buf, halo, spread, pack, square, b_packs, g_packs, log_send, log_recv, log_first, log_second, wide_decay,
+    bias, b_turned, halo, spread, pack, square, b_packs, g_packs, log_send, log_recv, log_first, log_second, wide_decay,
     keep, down_send, down_recv, top_send, top_recv, up_send, up_recv,
     halo_sems, log_sems, down_sems, top_sems, up_sems,
 ):
@@ -105,7 +105,7 @@
             log_copy(0).start()
         halo_copy.start()
         fill_spread(spread, heads)
-        state_ref[...] = jnp.zeros_like(state_ref)
+        bias[...] = 0.5 * bias_ref[...].reshape(1, bias.shape[1])
         ones = lower_triangle().astype(F32).T.astype(BF16)
         high, rest = split(logs)
         middle, low = split(rest)
@@ -126,55 +126,79 @@
             first, second = split(jnp.exp(mid))
             g_packs[8 * block : 8 * block + 8] = turned(first, second)
 
-    @pl.when(at < blocks - 1)
+    def halo_rows(source, block, inside, lanes):
+        if block == 0:
+            return jnp.where(place == 0, 0.0, halo[HALO : 2 * HALO, lanes].astype(F32))
+        return source[block * GROUP - 16 : block * GROUP, inside].astype(F32)[HALO:]
+
+    def mix(source, block, inside, outside):
+        pieces = []
+        for start in range(0, WIDE, LANES):
+            here = slice(inside + start, inside + start + LANES)
+            lanes = pl.ds(pl.multiple_of(outside + start, LANES), LANES)
+            span = slice(block * GROUP, (block + 1) * GROUP)
+            rows = jnp.concatenate(
+                [halo_rows(source, block, here, lanes), source[span, here].astype(F32)], axis=0
+            )
+            weights = 0.5 * weight_ref[:, lanes]
+            total = rows * weights[0:1]
+            for k in range(1, 4):
+                total = pltpu.roll(total, 1, 0) + rows * weights[k : k + 1]
+            part = total[HALO:] + bias[:, lanes]
+            pieces.append((part + part * jnp.tanh(part)).astype(BF16))
+        return jnp.concatenate(pieces, axis=1)
+
+    order = list(range(1, blocks)) + [0]
+
+    @pl.when(at == 0)
     def _():
-        buf[0:HALO] = before_ref[HALO : 2 * HALO].astype(F32)
-
-    for level in range(min(halvings, blocks - 2)):
-        @pl.when(at == level + 1)
+        for block in order:
+            if block == 0:
+                halo_copy.wait()
+            bc = mix(bc_in_ref, block, 0, inner)
+            bc_ref[block * GROUP : (block + 1) * GROUP] = bc
+            b_turned[block] = bc[:, : WIDE // 2].astype(F32).T.astype(BF16)
+
+    def widen(level):
+        decays = []
+        lane = lax.broadcasted_iota(jnp.int32, (8, LANES), 1)
+        for log in (log_first[level], log_second[level]):
+            first, second = split(jnp.exp(log))
+            decays.append(jnp.where(lane < half, first, pltpu.roll(second, half, 1)))
+        decay_pack = jnp.concatenate(decays, axis=0).astype(BF16)
+        for j in range(inner // WIDE):
+            columns = slice(j * WIDE, (j + 1) * WIDE)
+            wide_decay[16 * level : 16 * level + 16, columns] = dot(decay_pack, spread[:, columns])
+
+    for step_at in range(1, PARTS):
+        @pl.when(at == step_at)
         def _():
-            log_finish(level)
-
-    last = at == blocks - 1
-
-    @pl.when(last)
-    def _():
-        for level in range(min(halvings, blocks - 2), halvings):
-            log_finish(level)
-        halo_copy.wait()
-        buf[0:HALO] = jnp.where(place == 0, 0.0, halo[HALO : 2 * HALO].astype(F32))
-
-    block = lax.rem(at + 1, blocks)
-    b_pack = b_packs[pl.ds(pl.multiple_of(block * GROUP, GROUP), GROUP)]
-    g_pack = g_packs[pl.ds(pl.multiple_of(block * 8, 8), 8)].astype(BF16)
-
-    def mix(columns):
-        buf[HALO : HALO + GROUP, columns] = input_ref[:, columns].astype(F32)
-        total = bias_ref[columns].reshape(1, WIDE) + buf[HALO - 3 : HALO - 3 + GROUP, columns] * weight_ref[0:1, columns]
-        for k in range(1, 4):
-            total = total + buf[HALO - 3 + k : HALO - 3 + k + GROUP, columns] * weight_ref[k : k + 1, columns]
-        part = 0.5 * total
-        return (part + part * jnp.tanh(part)).astype(BF16)
-
-    bc = mix(slice(inner, inner + WIDE))
-    bc_ref[...] = bc
-    b_turned = bc[:, : WIDE // 2].astype(F32).T.astype(BF16)
-
-    def chunk(j):
-        columns = slice(j * WIDE, (j + 1) * WIDE)
+            stop = halvings if step_at == PARTS - 1 else min(step_at, halvings)
+            for level in range(min(step_at - 1, halvings), stop):
+                log_finish(level)
+                widen(level)
+
+    for j in range(inner // PARTS // WIDE):
+        outside = pl.multiple_of(at * (inner // PARTS) + j * WIDE, WIDE)
+        columns = pl.ds(outside, WIDE)
+        here = slice(j * WIDE, (j + 1) * WIDE)
         wide = spread[:, columns]
-        xb = (mix(columns).astype(F32) * dot(b_pack, wide)).astype(BF16)
-        xb_ref[:, columns] = xb
-        g8 = dot(g_pack, wide)
-        g_ref[:, columns] = g8
-        return columns, g8[0:1], dot(b_turned, xb)
-
-    @pl.when(at < blocks - 1)
-    def _():
-        for j in range(inner // WIDE):
-            columns, g, update = chunk(j)
-            state_ref[:, columns] = g * (g * state_ref[:, columns] + update)
-            wide_decay[0:8, columns] = jnp.where(at == 0, 1.0, wide_decay[0:8, columns]) * (g * g)
+        state, decay = None, None
+        for block in order:
+            span = slice(block * GROUP, (block + 1) * GROUP)
+            xb = (mix(input_ref, block, j * WIDE, outside).astype(F32) * dot(b_packs[span], wide)).astype(BF16)
+            xb_ref[span, here] = xb
+            g8 = dot(g_packs[8 * block : 8 * block + 8].astype(BF16), wide)
+            g_ref[8 * block : 8 * block + 8, here] = g8
+            g = g8[0:1]
+            update = g * dot(b_turned[block], xb)
+            if block == 0:
+                state = update if state is None else state + decay * update
+            elif state is None:
+                state, decay = update, g * g
+            else:
+                state, decay = (g * g) * state + update, decay * (g * g)
+        state_ref[:, columns] = state
 
     group = inner // PARTS
 
@@ -185,7 +209,7 @@
         return LANES >> (level + 1)
 
     def decay_row(level, which, columns):
-        row = 8 + 16 * level + 8 * which
+        row = 16 * level + 8 * which
         return wide_decay[row : row + 1, columns]
 
     def down_copy(level, part):
@@ -231,37 +255,36 @@
         state_ref[0:rows, columns] = jnp.where(right, got, mine)
         state_ref[rows : 2 * rows, columns] = jnp.where(right, mine, got)
 
-    @pl.when(last)
-    def _():
-        decays = []
-        for level in range(halvings):
-            for log in (log_first[level], log_second[level]):
-                first, second = split(jnp.exp(log))
-                lane = lax.broadcasted_iota(jnp.int32, (8, LANES), 1)
-                decays.append(jnp.where(lane < half, first, pltpu.roll(second, half, 1)))
-        decay_pack = jnp.concatenate(decays, axis=0).astype(BF16)
-        for j in range(inner // WIDE):
-            columns, g, update = chunk(j)
-            state_ref[:, columns] = state_ref[:, columns] + wide_decay[0:1, columns] * (g * update)
-            wide_decay[8 : 8 + 16 * halvings, columns] = dot(decay_pack, spread[:, columns])
-            for part in range(PARTS):
-                if (part + 1) * group == (j + 1) * WIDE:
-                    down_start(0, part)
-        for level in range(halvings):
-            for part in range(PARTS):
-                down_finish(level, part)
-                down_start(level + 1, part)
-        for part in range(PARTS):
+    rounds = 2 * halvings + 1
+
+    def advance(part, turn):
+        if turn < halvings:
+            down_finish(turn, part)
+            down_start(turn + 1, part)
+        elif turn == halvings:
             top_copy(part).wait()
             state_ref[0 : LANES >> halvings, part_of(part)] = jnp.where(
                 rights[levels - 1] == 1, top_recv[part].astype(F32), 0.0
             )
             up_start(halvings - 1, part)
-        for level in reversed(range(halvings)):
-            for part in range(PARTS):
-                up_finish(level, part)
-                if level > 0:
-                    up_start(level - 1, part)
+        else:
+            level = 2 * halvings - turn
+            up_finish(level, part)
+            if level > 0:
+                up_start(level - 1, part)
+
+    for step_at in range(PARTS):
+        @pl.when(at == step_at)
+        def _():
+            down_start(0, step_at)
+            for part in range(step_at):
+                if step_at - part - 1 < rounds:
+                    advance(part, step_at - part - 1)
+            if step_at == PARTS - 1:
+                for wave in range(rounds):
+                    for part in range(PARTS):
+                        if PARTS - 1 - part + wave < rounds:
+                            advance(part, PARTS - 1 - part + wave)
 
 
 def back_kernel(
@@ -319,8 +342,8 @@
     def stepped(*shape):
         return pl.BlockSpec(shape, lambda i: (i, 0))
 
-    def turned(*shape):
-        return pl.BlockSpec(shape, lambda i: (lax.rem(i + 1, blocks), 0))
+    def sideways(*shape):
+        return pl.BlockSpec(shape, lambda i: (0, i))
 
     def vmem(*shape, dtype=F32):
         return pltpu.VMEM(shape, dtype)
@@ -329,14 +352,14 @@
     shape = jax.ShapeDtypeStruct
     xb, bc, a, g, state = pl.pallas_call(
         functools.partial(front_kernel, inner, heads, blocks, count),
-        grid=(blocks,),
+        grid=(PARTS,),
         in_specs=[
-            pl.BlockSpec((16, conv_dim), lambda i: (jnp.maximum(lax.rem(i + 1, blocks) * (GROUP // 16) - 1, 0), 0)),
-            turned(GROUP, conv_dim), pl.BlockSpec(memory_space=pl.ANY),
+            sideways(tokens, group), pl.BlockSpec((tokens, WIDE), lambda i: (0, inner // WIDE)),
+            pl.BlockSpec(memory_space=pl.ANY),
             whole(heads, tokens), whole(4, conv_dim), whole(conv_dim), whole(heads), whole(heads),
         ],
         out_specs=[
-            turned(GROUP, inner), turned(GROUP, WIDE), whole(tokens, LANES), turned(8, inner),
+            sideways(tokens, group), whole(tokens, WIDE), whole(tokens, LANES), sideways(8 * blocks, group),
             whole(LANES, inner),
         ],
         out_shape=[
@@ -344,10 +367,10 @@
             shape((8 * blocks, inner), F32), shape((LANES, inner), F32),
         ],
         scratch_shapes=[
-            vmem(HALO + GROUP, conv_dim), vmem(16, conv_dim, dtype=BF16), vmem(LANES, inner, dtype=BF16),
+            vmem(1, conv_dim), vmem(blocks, LANES, GROUP, dtype=BF16), vmem(16, conv_dim, dtype=BF16), vmem(LANES, inner, dtype=BF16),
             vmem(LANES, GROUP), vmem(LANES, LANES), vmem(tokens, LANES, dtype=BF16), vmem(8 * blocks, LANES),
             vmem(halvings, 8, LANES), vmem(halvings, 8, LANES), vmem(halvings, 8, LANES), vmem(halvings, 8, LANES),
-            vmem(8 + 16 * halvings, inner),
+            vmem(16 * halvings, inner),
             [vmem(rows, inner) for rows in sizes], slots, slots,
             vmem(PARTS, LANES >> halvings, group, dtype=BF16), vmem(PARTS, LANES >> halvings, group, dtype=BF16),
             slots, slots,

time: 55.6 us -> 56.7 us (1.020)
  Pallas kernels: 55.4 us -> 56.5 us
    pallas_call x1, Pallas kernels: 44.9 us -> 46 us  [per_device(): pl.pallas_call(functools.partial(front_kernel, inner, heads, blocks, coun...]
where the time goes in v3:
time: 56.7 us; the launch traced here: 56.5 us
  Pallas kernels  56.5 us (100%)
    pallas_call x1, Pallas kernels, per_device(): pl.pallas_call(functools.partial(front_kernel, inner, heads, blocks, coun...  46 us
    pallas_call x1, Pallas kernels, per_device(): pl.pallas_call(functools.partial(back_kernel, inner, heads), grid=(blocks...  10.5 us

profile of v3, /device:TPU:0, one launch (start us, length us, event | category | flops | bytes accessed | tf_op | source)
XLA Modules:
  0.0 56.5 jit_solution(8645421656138540642)
XLA Ops:
  0.0 46.0 %front.1 = (bf16[1024,2560]{1,0:T(8,128)(2,1)}, bf16[1024,256]{1,0:T(8,128)(2,1)}, bf16[1024,128]{1,0:T(8,128)(2,1)}, f32[32,2560]{1,0:T(8,128)}, f32[128,2560]{1,0:T(8,128)}) custom-call(bf16[1024,2816]{1,0:T(8,128)(2,1)} %whole_ref.1, bf16[1024,2816]{1,0:T(8,128)(2,1)} %whole_ref.1, bf16[1024,2816]{1,0:T(8,128)(2,1)} %whole_ref.1, ...), custom_call_target="tpu_custom_call" | custom-call | tf_op jit(solution)/shard_map/front/pallas_call | solution.py:353
  46.0 10.5 %back.1 = bf16[1024,2560]{1,0:T(8,128)(2,1)} custom-call(bf16[1024,2560]{1,0:T(8,128)(2,1)} %get-tuple-element.10.xb_ref, bf16[1024,256]{1,0:T(8,128)(2,1)} %get-tuple-element.11.bc_ref, bf16[1024,128]{1,0:T(8,128)(2,1)} %get-tuple-element.12.a_ref, f32[32,2560]{1,0:T(8,128)} %get-tuple-element.13.g_ref, f32[128,2560]{1,0:T(8,128)} %get-tuple-element.14.incoming_ref, ...), custom_call_target="tpu_custom_call" | custom-call | tf_op jit(solution)/shard_map/back/pallas_call | solution.py:384

commit v4 on v2

--- a/solution.py
+++ b/solution.py
@@ -149,12 +149,17 @@
     g_pack = g_packs[pl.ds(pl.multiple_of(block * 8, 8), 8)].astype(BF16)
 
     def mix(columns):
-        buf[HALO : HALO + GROUP, columns] = input_ref[:, columns].astype(F32)
-        total = bias_ref[columns].reshape(1, WIDE) + buf[HALO - 3 : HALO - 3 + GROUP, columns] * weight_ref[0:1, columns]
-        for k in range(1, 4):
-            total = total + buf[HALO - 3 + k : HALO - 3 + k + GROUP, columns] * weight_ref[k : k + 1, columns]
-        part = 0.5 * total
-        return (part + part * jnp.tanh(part)).astype(BF16)
+        pieces = []
+        for start in range(columns.start, columns.stop, LANES):
+            lanes = slice(start, start + LANES)
+            rows = jnp.concatenate([buf[0:HALO, lanes], input_ref[:, lanes].astype(F32)], axis=0)
+            weights = 0.5 * weight_ref[:, lanes]
+            total = rows * weights[0:1]
+            for k in range(1, 4):
+                total = pltpu.roll(total, 1, 0) + rows * weights[k : k + 1]
+            part = total[HALO:] + 0.5 * bias_ref[lanes].reshape(1, LANES)
+            pieces.append((part + part * jnp.tanh(part)).astype(BF16))
+        return jnp.concatenate(pieces, axis=1)
 
     bc = mix(slice(inner, inner + WIDE))
     bc_ref[...] = bc
@@ -344,7 +349,7 @@
             shape((8 * blocks, inner), F32), shape((LANES, inner), F32),
         ],
         scratch_shapes=[
-            vmem(HALO + GROUP, conv_dim), vmem(16, conv_dim, dtype=BF16), vmem(LANES, inner, dtype=BF16),
+            vmem(HALO, conv_dim), vmem(16, conv_dim, dtype=BF16), vmem(LANES, inner, dtype=BF16),
             vmem(LANES, GROUP), vmem(LANES, LANES), vmem(tokens, LANES, dtype=BF16), vmem(8 * blocks, LANES),
             vmem(halvings, 8, LANES), vmem(halvings, 8, LANES), vmem(halvings, 8, LANES), vmem(halvings, 8, LANES),
             vmem(8 + 16 * halvings, inner),

time: 55.6 us -> 51.5 us (0.926)
  Pallas kernels: 55.4 us -> 51.3 us
    pallas_call x1, Pallas kernels: 44.9 us -> 40.8 us  [per_device(): pl.pallas_call(functools.partial(front_kernel, inner, heads, blocks, coun...]
where the time goes in v4:
time: 51.5 us; the launch traced here: 51.3 us
  Pallas kernels  51.3 us (100%)
    pallas_call x1, Pallas kernels, per_device(): pl.pallas_call(functools.partial(front_kernel, inner, heads, blocks, coun...  40.8 us
    pallas_call x1, Pallas kernels, per_device(): pl.pallas_call(functools.partial(back_kernel, inner, heads), grid=(blocks...  10.5 us

profile of v4, /device:TPU:0, one launch (start us, length us, event | category | flops | bytes accessed | tf_op | source)
XLA Modules:
  0.0 51.3 jit_solution(5262693450861254592)
XLA Ops:
  0.0 40.8 %front.1 = (bf16[1024,2560]{1,0:T(8,128)(2,1)}, bf16[1024,256]{1,0:T(8,128)(2,1)}, bf16[1024,128]{1,0:T(8,128)(2,1)}, f32[32,2560]{1,0:T(8,128)}, f32[128,2560]{1,0:T(8,128)}) custom-call(bf16[1024,2816]{1,0:T(8,128)(2,1)} %whole_ref.1, bf16[1024,2816]{1,0:T(8,128)(2,1)} %whole_ref.1, bf16[1024,2816]{1,0:T(8,128)(2,1)} %whole_ref.1, ...), custom_call_target="tpu_custom_call" | custom-call | tf_op jit(solution)/shard_map/front/pallas_call | solution.py:335
  40.8 10.5 %back.1 = bf16[1024,2560]{1,0:T(8,128)(2,1)} custom-call(bf16[1024,2560]{1,0:T(8,128)(2,1)} %get-tuple-element.10.xb_ref, bf16[1024,256]{1,0:T(8,128)(2,1)} %get-tuple-element.11.bc_ref, bf16[1024,128]{1,0:T(8,128)(2,1)} %get-tuple-element.12.a_ref, f32[32,2560]{1,0:T(8,128)} %get-tuple-element.13.g_ref, f32[128,2560]{1,0:T(8,128)} %get-tuple-element.14.incoming_ref, ...), custom_call_target="tpu_custom_call" | custom-call | tf_op jit(solution)/shard_map/back/pallas_call | solution.py:366
